TPU v7x, 1024 devices: a whole 8x8x8 slice. The times are simulated.
1024 devices in a mesh: trench: 64 (over y, z_lo, core), tblock: 16 (over z_hi, x).
Axes of the slice: x: 8, y: 8, z: 8 (z_hi: 2, z_lo: 4; z = z_hi * 4 + z_lo), core: 2. Of those that a mesh axis runs over, the one named last changes fastest.
Arguments:
- adjoint_eta: float32 [16, 30, 1024, 512], P('tblock', None, 'trench'), may hold values from -6 to 6
- adjoint_flow: float32 [16, 30, 1024, 512], P('tblock', None, 'trench'), may hold values from -6 to 6
- residual: float32 [16, 64, 64, 4, 32], P('tblock', 'trench'), may hold values from -6 to 6
- sensor_cell: int32 [64, 64, 32], replicated, may hold values from 0 to 8191
- sensor_count: int32 [64, 64], replicated, may hold values from 0 to 32, as said below
- depth_class: int32 [1024, 512], P('trench'), may hold values from 0 to 7
- speed_table: float32 [8], replicated, may hold values from 0.1 to 0.3
- damping: float32 [30], replicated, may hold values from 0.6 to 1
- profile: float32 [30], replicated, may hold values from 0.3 to 1
- band_weight: float32 [8], replicated, may hold values from 0.3 to 1
Outputs:
- uplift_grad: float32 [64, 1024, 512], P(None, ('trench', 'tblock'))
Inputs may be any that keep to these rules, and one draw needn't show every extreme that they name: `sensor_cell`: column index inside the owning tile, row times 512 plus column. `sensor_count`: in every draw some owning tile receives 32 live slots from every source tile.
All inputs are finite; a program needn't handle non-finite values.
Results may differ from a plain program's by a relative error of at most 0.0001.
Values sent between devices are 32-bit elements; how exact they have to be, the bound alone decides.
A program may use at most 32 MiB of HBM per device.

v0:
```python
import math

import jax
import jax.numpy as jnp
from jax import lax
from jax.sharding import PartitionSpec as P

VERT = 0.2


def with_halo(x, sides, width):
    for axis, dim in sides:
        devices, length = (lax.axis_size(axis), x.shape[dim])
        up = [(i, (i + 1) % devices) for i in range(devices - 1)]
        down = [(j, i) for i, j in up]
        last = lax.slice_in_dim(x, length - width, length, axis=dim)
        initial = lax.slice_in_dim(x, 0, width, axis=dim)
        before = lax.ppermute(last, axis, up)
        after = lax.ppermute(initial, axis, down)
        x = jnp.concatenate([before, x, after], axis=dim)
    return x


def lookup(depth_class, speed_table):
    classes = jnp.arange(speed_table.shape[0], dtype=jnp.int32)
    return jnp.sum(
        jnp.where(depth_class[..., None] == classes, speed_table, jnp.float32(0.0)), axis=-1
    )


def advance(widened, displace, momentum, celerity, inject, damping):
    across_pad = jnp.pad(displace, ((0, 0), (0, 0), (1, 1)))
    laplace = (
        widened[:, 2:]
        + widened[:, :-2]
        + across_pad[:, :, 2:]
        + across_pad[:, :, :-2]
        - 4.0 * displace
    )
    level_pad = jnp.pad(displace, ((1, 1), (0, 0), (0, 0)))
    vertical = level_pad[2:] + level_pad[:-2] - 2.0 * displace
    levels = displace.shape[0]
    bottom = (jnp.arange(levels, dtype=jnp.int32) == levels - 1).astype(jnp.float32)
    momentum = (
        damping[:, None, None] * momentum
        + celerity[None] * laplace
        + VERT * vertical
        + bottom[:, None, None] * inject[None]
    )
    return (displace + momentum, momentum)


def prior(series, band_weight):
    width_band = band_weight.shape[0]
    length = series.shape[0]
    padded = jnp.pad(series, ((0, width_band - 1), (0, 0), (0, 0)))
    result = jnp.zeros_like(series)
    for offset in range(width_band):
        result = result + band_weight[offset] * padded[offset : offset + length]
    return result


def body(
    adjoint_eta,
    adjoint_flow,
    residual,
    sensor_cell,
    sensor_count,
    depth_class,
    speed_table,
    damping,
    profile,
    band_weight,
):
    mine = lax.axis_index("trench")
    levels = adjoint_eta.shape[1]
    rows = adjoint_eta.shape[2]
    across = adjoint_eta.shape[3]
    steps_count = residual.shape[3]
    level_scale = 1.0 / math.sqrt(levels)
    outgoing = residual[0, 0]
    incoming = lax.all_to_all(outgoing, "trench", split_axis=0, concat_axis=0, tiled=True)
    my_cells = lax.dynamic_slice_in_dim(sensor_cell, mine, 1, 1)[:, 0, :]
    my_counts = lax.dynamic_slice_in_dim(sensor_count, mine, 1, 1)[:, 0]
    slot_ids = jnp.arange(incoming.shape[2], dtype=jnp.int32)
    alive_mask = (slot_ids[None, :] < my_counts[:, None]).astype(jnp.float32)
    values = jnp.transpose(incoming * alive_mask[:, None, :], (1, 0, 2)).reshape(steps_count, -1)
    target = my_cells.reshape(-1)
    inject_all = (
        jnp.zeros((steps_count, rows * across), jnp.float32)
        .at[:, target]
        .add(values)
        .reshape(steps_count, rows, across)
    )
    celerity = lookup(depth_class, speed_table)
    displace = adjoint_eta[0]
    momentum = adjoint_flow[0]
    pieces = [None] * steps_count
    for step_back in range(steps_count):
        moment = steps_count - 1 - step_back
        widened = with_halo(displace, (("trench", 1),), 1)
        displace, momentum = advance(
            widened, displace, momentum, celerity, inject_all[moment], damping
        )
        pieces[moment] = jnp.sum(profile[:, None, None] * momentum, axis=0) * level_scale
    local_series = jnp.stack(pieces, 0)
    return prior(
        lax.all_to_all(local_series, "tblock", split_axis=1, concat_axis=0, tiled=True), band_weight
    )


def solution(mesh):
    in_specs = (
        P("tblock", None, "trench", None),
        P("tblock", None, "trench", None),
        P("tblock", "trench", None, None, None),
        P(),
        P(),
        P("trench", None),
        P(),
        P(),
        P(),
        P(),
    )
    out_specs = P(None, ("trench", "tblock"), None)
    return jax.shard_map(body, mesh=mesh, in_specs=in_specs, out_specs=out_specs, check_vma=False)
```

profile of v0, /device:TPU:64, one launch (start us, length us, event | category | flops | bytes accessed | tf_op | source)
XLA Modules:
  0.0 157.6 jit_solution(7345367061376999645)
XLA Ops:
  0.0 0.0 copy-start
  0.0 1.0 copy.25
  1.0 0.8 reshape.133
  1.8 16.5 %all-to-all-start = ((f32[64,1,128]{2,1,0:T(1,128)}), f32[64,1,128]{2,1,0:T(1,128)S(1)}, u32[]{:S(2)}, u32[]{:S(2)}) async-start(f32[64,1,128]{2,1,0:T(1,128)} %reshape.133), calls=%async_computation | async-start | bytes 65536 | tf_op jit(solution)/shard_map/all_to_all | solution.py:82
  18.3 1.3 fusion.57
  19.6 4.9 %collective-permute-start = (f32[30,1,512]{2,1,0:T(1,128)S(1)}, f32[30,1,512]{2,1,0:T(1,128)S(1)}, u32[]{:S(2)}, u32[]{:S(2)}) collective-permute-start(f32[30,1,512]{2,1,0:T(1,128)S(1)} %get-tuple-element.25), channel_id=1, source_target_pairs={{16,0},{32,16},{48,32},{64,48},{80,64},{96,80},{112,96},{128,112},... | collective-permute-start | bytes 184328 | tf_op jit(solution)/shard_map/ppermute | solution.py:19
  24.6 1.9 %collective-permute-start.1 = (f32[30,1,512]{2,1,0:T(1,128)S(1)}, f32[30,1,512]{2,1,0:T(1,128)S(1)}, u32[]{:S(2)}, u32[]{:S(2)}) collective-permute-start(f32[30,1,512]{2,1,0:T(1,128)S(1)} %get-tuple-element.26), channel_id=1, source_target_pairs={{0,16},{16,32},{32,48},{48,64},{64,80},{80,96},{96,112},{112,128},... | collective-permute-start | bytes 184328 | tf_op jit(solution)/shard_map/ppermute | solution.py:18
  26.5 0.9 dynamic-slice_reduce_fusion.1
  27.4 0.1 fusion.48
  27.5 0.0 copy-done
  27.5 1.4 dynamic-slice_reduce_fusion
  29.0 0.1 reshape_squeeze.3
  29.1 0.9 select_reduce_fusion
  30.0 0.0 all-to-all-done
  30.0 0.5 broadcast.142
  30.5 0.7 reduce.12
  31.3 0.1 reshape.134
  31.5 0.1 reshape.118
  31.6 0.4 copy.27
  31.9 13.6 %scatter_custom_fusion = f32[4,8192]{0,1:T(8,128)} fusion(s32[2048]{0:T(1024)S(1)} %bitcast.36, f32[2048,4]{1,0:T(8,128)S(1)} %copy.27, f32[]{:T(128)} %constant.11.clone.1), kind=kCustom, calls=%fused_computation.5 | custom fusion | flops 8192 | bytes 131076 | tf_op jit(solution)/shard_map/scatter-add | solution.py:92
  45.6 0.0 copy-start.1
  45.6 0.0 copy-start.6
  45.6 14.0 %slice_reduce_fusion = (f32[8192]{0:T(1024)S(1)}, f32[8192]{0:T(1024)S(1)}, f32[8192]{0:T(1024)S(1)}, f32[8192]{0:T(1024)S(1)}) fusion(f32[4,8192]{0,1:T(8,128)} %scatter_custom_fusion), kind=kLoop, calls=%fused_computation.1 | loop fusion | bytes 262144 | tf_op jit(solution)/shard_map/slice | solution.py:103
  59.6 0.0 collective-permute-done
  59.6 0.0 collective-permute-done.1
  59.6 0.0 copy-done.1
  59.7 0.0 copy-done.6
  59.7 2.3 %bitcast_add_fusion = (f32[30,16,512]{2,1,0:T(8,128)S(1)}, f32[30,16,512]{2,1,0:T(8,128)S(1)}) fusion(f32[1,30,16,512]{3,2,1,0:T(8,128)S(1)} %copy-done.1, f32[16,512]{1,0:T(8,128)S(1)} %mul.302, f32[30]{0:T(128)S(1)} %compare_convert_fusion, f32[30,16,512]{2,1,0:T(8,128)S(1)} %bitcast.32, f32[30,1,512]{2,1,0:T(1,128)S(1)} %collective-permute-done.1, ...), kind=kLoop, calls=%fused_computation.96 | loop fusion | flops 4423680 | bytes 5103856 | tf_op jit(solution)/shard_map/add | solution.py:50
  62.0 0.0 copy-start.4
  62.0 0.9 copy-done.4
  62.9 0.1 fusion.56
  63.0 7.5 %collective-permute-start.2 = (f32[30,1,512]{2,1,0:T(1,128)S(1)}, f32[30,1,512]{2,1,0:T(1,128)S(1)}, u32[]{:S(2)}, u32[]{:S(2)}) collective-permute-start(f32[30,1,512]{2,1,0:T(1,128)S(1)} %get-tuple-element.23), channel_id=1, source_target_pairs={{16,0},{32,16},{48,32},{64,48},{80,64},{96,80},{112,96},{128,112},... | collective-permute-start | bytes 184328 | tf_op jit(solution)/shard_map/ppermute | solution.py:19
  70.6 2.1 %collective-permute-start.3 = (f32[30,1,512]{2,1,0:T(1,128)S(1)}, f32[30,1,512]{2,1,0:T(1,128)S(1)}, u32[]{:S(2)}, u32[]{:S(2)}) collective-permute-start(f32[30,1,512]{2,1,0:T(1,128)S(1)} %get-tuple-element.24), channel_id=1, source_target_pairs={{0,16},{16,32},{32,48},{48,64},{64,80},{80,96},{96,112},{112,128},... | collective-permute-start | bytes 184328 | tf_op jit(solution)/shard_map/ppermute | solution.py:18
  72.7 0.0 collective-permute-done.2
  72.7 7.3 %collective-permute-done.3 = f32[30,1,512]{2,1,0:T(1,128)S(1)} collective-permute-done((f32[30,1,512]{2,1,0:T(1,128)S(1)}, f32[30,1,512]{2,1,0:T(1,128)S(1)}, u32[]{:S(2)}, u32[]{:S(2)}) %collective-permute-start.3) | collective-permute-done | bytes 61472 | tf_op jit(solution)/shard_map/ppermute | solution.py:18
  80.0 0.0 copy-start.7
  80.0 5.0 %fusion.51 = (f32[30,16,512]{2,1,0:T(8,128)S(1)}, f32[30,16,512]{2,1,0:T(8,128)S(1)}) fusion(f32[30,16,512]{2,1,0:T(8,128)} %copy-done.4, f32[16,512]{1,0:T(8,128)S(1)} %mul.310, f32[30]{0:T(128)S(1)} %compare_convert_fusion, f32[30,1,512]{2,1,0:T(1,128)S(1)} %collective-permute-done.3, f32[30,1,512]{2,1,0:T(1,128)S(1)} %collective-permute-done.2, ...), kind=kLoop, calls=%fused_computation.98 | loop fusion | flops 4423680 | bytes 4120816 | tf_op jit(solution)/shard_map/add | solution.py:50
  85.1 0.0 copy-start.3
  85.1 1.0 copy-done.3
  86.1 0.1 fusion.55
  86.2 1.9 %collective-permute-start.4 = (f32[30,1,512]{2,1,0:T(1,128)S(1)}, f32[30,1,512]{2,1,0:T(1,128)S(1)}, u32[]{:S(2)}, u32[]{:S(2)}) collective-permute-start(f32[30,1,512]{2,1,0:T(1,128)S(1)} %get-tuple-element.21), channel_id=1, source_target_pairs={{16,0},{32,16},{48,32},{64,48},{80,64},{96,80},{112,96},{128,112},... | collective-permute-start | bytes 184328 | tf_op jit(solution)/shard_map/ppermute | solution.py:19
  88.1 2.4 %collective-permute-start.5 = (f32[30,1,512]{2,1,0:T(1,128)S(1)}, f32[30,1,512]{2,1,0:T(1,128)S(1)}, u32[]{:S(2)}, u32[]{:S(2)}) collective-permute-start(f32[30,1,512]{2,1,0:T(1,128)S(1)} %get-tuple-element.22), channel_id=1, source_target_pairs={{0,16},{16,32},{32,48},{48,64},{64,80},{80,96},{96,112},{112,128},... | collective-permute-start | bytes 184328 | tf_op jit(solution)/shard_map/ppermute | solution.py:18
  90.5 0.0 collective-permute-done.4
  90.5 7.0 %collective-permute-done.5 = f32[30,1,512]{2,1,0:T(1,128)S(1)} collective-permute-done((f32[30,1,512]{2,1,0:T(1,128)S(1)}, f32[30,1,512]{2,1,0:T(1,128)S(1)}, u32[]{:S(2)}, u32[]{:S(2)}) %collective-permute-start.5) | collective-permute-done | bytes 61472 | tf_op jit(solution)/shard_map/ppermute | solution.py:18
  97.5 0.0 copy-start.5
  97.6 6.3 %fusion.49 = (f32[30,16,512]{2,1,0:T(8,128)S(1)}, f32[30,16,512]{2,1,0:T(8,128)}) fusion(f32[30,16,512]{2,1,0:T(8,128)} %copy-done.3, f32[16,512]{1,0:T(8,128)S(1)} %mul.318, f32[30]{0:T(128)S(1)} %compare_convert_fusion, f32[30,1,512]{2,1,0:T(1,128)S(1)} %collective-permute-done.5, f32[30,1,512]{2,1,0:T(1,128)S(1)} %collective-permute-done.4, ...), kind=kLoop, calls=%fused_computation.97 | loop fusion | flops 4423680 | bytes 4120816 | tf_op jit(solution)/shard_map/add | solution.py:50
  103.8 0.0 copy-start.2
  103.8 1.0 copy-done.2
  104.8 0.1 fusion.54
  104.9 1.9 %collective-permute-start.6 = (f32[30,1,512]{2,1,0:T(1,128)S(1)}, f32[30,1,512]{2,1,0:T(1,128)S(1)}, u32[]{:S(2)}, u32[]{:S(2)}) collective-permute-start(f32[30,1,512]{2,1,0:T(1,128)S(1)} %get-tuple-element.19), channel_id=1, source_target_pairs={{16,0},{32,16},{48,32},{64,48},{80,64},{96,80},{112,96},{128,112},... | collective-permute-start | bytes 184328 | tf_op jit(solution)/shard_map/ppermute | solution.py:19
  106.9 2.4 %collective-permute-start.7 = (f32[30,1,512]{2,1,0:T(1,128)S(1)}, f32[30,1,512]{2,1,0:T(1,128)S(1)}, u32[]{:S(2)}, u32[]{:S(2)}) collective-permute-start(f32[30,1,512]{2,1,0:T(1,128)S(1)} %get-tuple-element.20), channel_id=1, source_target_pairs={{0,16},{16,32},{32,48},{48,64},{64,80},{80,96},{96,112},{112,128},... | collective-permute-start | bytes 184328 | tf_op jit(solution)/shard_map/ppermute | solution.py:18
  109.3 0.0 collective-permute-done.6
  109.3 7.0 %collective-permute-done.7 = f32[30,1,512]{2,1,0:T(1,128)S(1)} collective-permute-done((f32[30,1,512]{2,1,0:T(1,128)S(1)}, f32[30,1,512]{2,1,0:T(1,128)S(1)}, u32[]{:S(2)}, u32[]{:S(2)}) %collective-permute-start.7) | collective-permute-done | bytes 61472 | tf_op jit(solution)/shard_map/ppermute | solution.py:18
  116.3 0.0 copy-done.7
  116.3 5.8 %fusion.23 = (f32[16,512]{1,0:T(8,128)S(1)}, f32[16,512]{1,0:T(8,128)S(1)}, f32[16,512]{1,0:T(8,128)S(1)}, f32[16,512]{1,0:T(8,128)S(1)}) fusion(f32[30,16,512]{2,1,0:T(8,128)} %copy-done.2, f32[30,1,512]{2,1,0:T(1,128)S(1)} %collective-permute-done.7, f32[30,1,512]{2,1,0:T(1,128)S(1)} %collective-permute-done.6, f32[30,16,512]{2,1,0:T(8,128)} %get-tuple-element.14, ...), kind=kLoop, calls=%fused_computation.45 | loop fusion | flops 6111232 | bytes 4252008 | tf_op jit(solution)/shard_map/reduce_sum | solution.py:105
  122.3 0.8 pad_maximum_fusion.8
  123.1 15.7 %all-to-all-start.1 = ((f32[4,16,512]{2,0,1:T(4,128)}), f32[4,16,512]{2,0,1:T(4,128)S(1)}, u32[]{:S(2)}, u32[]{:S(2)}) async-start(f32[4,16,512]{2,0,1:T(4,128)} %pad_maximum_fusion.8), calls=%async_computation.1 | async-start | bytes 262144 | tf_op jit(solution)/shard_map/all_to_all | solution.py:108
  138.9 0.0 copy-done.5
  138.9 0.7 fusion.58
  139.6 11.8 %all-to-all-done.1 = f32[4,16,512]{2,0,1:T(4,128)S(1)} async-done(((f32[4,16,512]{2,0,1:T(4,128)}), f32[4,16,512]{2,0,1:T(4,128)S(1)}, u32[]{:S(2)}, u32[]{:S(2)}) %all-to-all-start.1) | async-done | bytes 131104 | tf_op jit(solution)/shard_map/all_to_all | solution.py:108
  151.3 0.1 all_to_all.18
  151.4 6.1 %multiply_add_fusion = f32[64,1,512]{2,1,0:T(1,128)} fusion(f32[64,1,512]{2,1,0:T(1,128)S(1)} %bitcast.34, f32[]{:T(128)} %bitcast.19, f32[]{:T(128)} %bitcast.18, f32[]{:T(128)} %bitcast.17, f32[]{:T(128)} %bitcast.16, f32[]{:T(128)} %bitcast.15, f32[]{:T(128)} %bitcast.14, f32[]{:T(128)} %bitcast.12, f32[]{:T(128)} %bitcast), kind=kLoop, calls=%fused_computation.85 | loop fusion | flops 491520 | bytes 262176 | tf_op jit(solution)/shard_map/add | solution.py:59
  (15 shorter events, 0.2 us)
Async XLA Ops:
  0.0 27.5 %copy-start = (s32[64,64,32]{1,2,0:T(8,128)S(1)}, s32[64,64,32]{1,2,0:T(8,128)}, u32[]{:S(2)}) copy-start(s32[64,64,32]{1,2,0:T(8,128)} %param.13) | copy-start | bytes 1572868
  1.8 28.2 %all-to-all-start = ((f32[64,1,128]{2,1,0:T(1,128)}), f32[64,1,128]{2,1,0:T(1,128)S(1)}, u32[]{:S(2)}, u32[]{:S(2)}) async-start(f32[64,1,128]{2,1,0:T(1,128)} %reshape.133), calls=%async_computation | async-start | bytes 65536 | tf_op jit(solution)/shard_map/all_to_all | solution.py:82
  19.6 40.0 %collective-permute-start = (f32[30,1,512]{2,1,0:T(1,128)S(1)}, f32[30,1,512]{2,1,0:T(1,128)S(1)}, u32[]{:S(2)}, u32[]{:S(2)}) collective-permute-start(f32[30,1,512]{2,1,0:T(1,128)S(1)} %get-tuple-element.25), channel_id=1, source_target_pairs={{16,0},{32,16},{48,32},{64,48},{80,64},{96,80},{112,96},{128,112},... | collective-permute-start | bytes 184328 | tf_op jit(solution)/shard_map/ppermute | solution.py:19
  24.6 35.1 %collective-permute-start.1 = (f32[30,1,512]{2,1,0:T(1,128)S(1)}, f32[30,1,512]{2,1,0:T(1,128)S(1)}, u32[]{:S(2)}, u32[]{:S(2)}) collective-permute-start(f32[30,1,512]{2,1,0:T(1,128)S(1)} %get-tuple-element.26), channel_id=1, source_target_pairs={{0,16},{16,32},{32,48},{48,64},{64,80},{80,96},{96,112},{112,128},... | collective-permute-start | bytes 184328 | tf_op jit(solution)/shard_map/ppermute | solution.py:18
  45.6 14.1 %copy-start.1 = (f32[1,30,16,512]{3,2,1,0:T(8,128)S(1)}, f32[1,30,16,512]{3,2,1,0:T(8,128)}, u32[]{:S(2)}) copy-start(f32[1,30,16,512]{3,2,1,0:T(8,128)} %param.10) | copy-start | bytes 2949124
  45.6 14.1 %copy-start.6 = (f32[30]{0:T(128)S(1)}, f32[30]{0:T(128)}, u32[]{:S(2)}) copy-start(f32[30]{0:T(128)} %param.17) | copy-start | bytes 364
  62.0 1.0 copy-start.4
  63.0 9.7 %collective-permute-start.2 = (f32[30,1,512]{2,1,0:T(1,128)S(1)}, f32[30,1,512]{2,1,0:T(1,128)S(1)}, u32[]{:S(2)}, u32[]{:S(2)}) collective-permute-start(f32[30,1,512]{2,1,0:T(1,128)S(1)} %get-tuple-element.23), channel_id=1, source_target_pairs={{16,0},{32,16},{48,32},{64,48},{80,64},{96,80},{112,96},{128,112},... | collective-permute-start | bytes 184328 | tf_op jit(solution)/shard_map/ppermute | solution.py:19
  70.6 9.4 %collective-permute-start.3 = (f32[30,1,512]{2,1,0:T(1,128)S(1)}, f32[30,1,512]{2,1,0:T(1,128)S(1)}, u32[]{:S(2)}, u32[]{:S(2)}) collective-permute-start(f32[30,1,512]{2,1,0:T(1,128)S(1)} %get-tuple-element.24), channel_id=1, source_target_pairs={{0,16},{16,32},{32,48},{48,64},{64,80},{80,96},{96,112},{112,128},... | collective-permute-start | bytes 184328 | tf_op jit(solution)/shard_map/ppermute | solution.py:18
  80.0 36.3 %copy-start.7 = (f32[30]{0:T(128)S(1)}, f32[30]{0:T(128)}, u32[]{:S(2)}) copy-start(f32[30]{0:T(128)} %param.18) | copy-start | bytes 364
  85.1 1.0 copy-start.3
  86.2 4.4 %collective-permute-start.4 = (f32[30,1,512]{2,1,0:T(1,128)S(1)}, f32[30,1,512]{2,1,0:T(1,128)S(1)}, u32[]{:S(2)}, u32[]{:S(2)}) collective-permute-start(f32[30,1,512]{2,1,0:T(1,128)S(1)} %get-tuple-element.21), channel_id=1, source_target_pairs={{16,0},{32,16},{48,32},{64,48},{80,64},{96,80},{112,96},{128,112},... | collective-permute-start | bytes 184328 | tf_op jit(solution)/shard_map/ppermute | solution.py:19
  88.1 9.4 %collective-permute-start.5 = (f32[30,1,512]{2,1,0:T(1,128)S(1)}, f32[30,1,512]{2,1,0:T(1,128)S(1)}, u32[]{:S(2)}, u32[]{:S(2)}) collective-permute-start(f32[30,1,512]{2,1,0:T(1,128)S(1)} %get-tuple-element.22), channel_id=1, source_target_pairs={{0,16},{16,32},{32,48},{48,64},{64,80},{80,96},{96,112},{112,128},... | collective-permute-start | bytes 184328 | tf_op jit(solution)/shard_map/ppermute | solution.py:18
  97.5 41.3 %copy-start.5 = (f32[8]{0:T(128)S(1)}, f32[8]{0:T(128)}, u32[]{:S(2)}) copy-start(f32[8]{0:T(128)} %param.19) | copy-start | bytes 100
  103.8 1.0 copy-start.2
  104.9 4.4 %collective-permute-start.6 = (f32[30,1,512]{2,1,0:T(1,128)S(1)}, f32[30,1,512]{2,1,0:T(1,128)S(1)}, u32[]{:S(2)}, u32[]{:S(2)}) collective-permute-start(f32[30,1,512]{2,1,0:T(1,128)S(1)} %get-tuple-element.19), channel_id=1, source_target_pairs={{16,0},{32,16},{48,32},{64,48},{80,64},{96,80},{112,96},{128,112},... | collective-permute-start | bytes 184328 | tf_op jit(solution)/shard_map/ppermute | solution.py:19
  106.9 9.4 %collective-permute-start.7 = (f32[30,1,512]{2,1,0:T(1,128)S(1)}, f32[30,1,512]{2,1,0:T(1,128)S(1)}, u32[]{:S(2)}, u32[]{:S(2)}) collective-permute-start(f32[30,1,512]{2,1,0:T(1,128)S(1)} %get-tuple-element.20), channel_id=1, source_target_pairs={{0,16},{16,32},{32,48},{48,64},{64,80},{80,96},{96,112},{112,128},... | collective-permute-start | bytes 184328 | tf_op jit(solution)/shard_map/ppermute | solution.py:18
  123.1 28.2 %all-to-all-start.1 = ((f32[4,16,512]{2,0,1:T(4,128)}), f32[4,16,512]{2,0,1:T(4,128)S(1)}, u32[]{:S(2)}, u32[]{:S(2)}) async-start(f32[4,16,512]{2,0,1:T(4,128)} %pad_maximum_fusion.8), calls=%async_computation.1 | async-start | bytes 262144 | tf_op jit(solution)/shard_map/all_to_all | solution.py:108
where the time goes:
time: 158 us
  starting transfers between devices  57.4 us (36%)
  other arithmetic  41.7 us (26%)
  waiting for transfers between devices  33.1 us (21%)
  local copies, waits for them, and re-layouts  24.9 us (16%)
    ppermute x4, waiting for transfers between devices, with_halo(): before = lax.ppermute(last, axis, up)  21.3 us
    all_to_all x1, starting transfers between devices, body(): lax.all_to_all(outgoing, 'trench', split_axis=0, concat_axis=0, tiled=True)  16.5 us
    ppermute x4, starting transfers between devices, with_halo(): after = lax.ppermute(initial, axis, down)  16.3 us
    all_to_all x1, starting transfers between devices, body(): lax.all_to_all(local_series, 'tblock', split_axis=1, concat_axis=0, tiled...  15.7 us
    slice x1, local copies, waits for them, and re-layouts, body(): inject_all[moment]  14 us
    add x3, other arithmetic, advance(): return (displace + momentum, momentum)  13.6 us
    scatter-add x1, other arithmetic, body(): inject_all = jnp.zeros((steps_count, rows * across), jnp.float32).at[:, t...  13.6 us
    all_to_all x1, waiting for transfers between devices, body(): lax.all_to_all(local_series, 'tblock', split_axis=1, concat_axis=0, tiled...  11.8 us
  transfers between devices with their start and end apart: 10, of which 4 were waited for; matrix products, arithmetic and copies ran while one was open for 22% of the time, Pallas kernels for 0%

commit v1 on v0

v1 whole, which is shorter than its diff:
```python
import functools
import math

import jax
import jax.numpy as jnp
from jax import lax
from jax.experimental import pallas as pl
from jax.experimental.pallas import tpu as pltpu
from jax.sharding import PartitionSpec as P

VERT = 0.2
MESH = pl.DeviceIdType.MESH
LANES = 128
SUB = 8
PHASES = 3
RING = PHASES * SUB
SLOTS = 64


def divisor(count, limit):
    return max(size for size in range(1, limit + 1) if count % size == 0)


def kernel(
    cfg,
    eta,
    flow,
    residual,
    cells,
    counts,
    depth,
    speed,
    damping,
    profile,
    band,
    out,
    disp,
    mom,
    res_buf,
    cell_buf,
    depth_own,
    depth_low,
    depth_high,
    depth_ring,
    coef,
    msg,
    recv,
    onehot_row,
    onehot_col,
    cols,
    inject,
    acc_ref,
    send_rows,
    rows_in,
    edge_in,
    total,
    load_sem,
    depth_send,
    depth_recv,
    res_send,
    res_recv,
    row_send,
    row_recv,
    edge_send,
    edge_recv,
):
    tiles, windows, levels, rows, blocks, steps, cap = cfg
    own = lax.axis_index("trench")
    win = lax.axis_index("tblock")
    f32 = jnp.float32
    reach = steps
    part = steps * blocks
    half = cap // 2

    loads = []
    for j in range(blocks):
        lanes = pl.ds(j * LANES, LANES)
        loads.append(
            pltpu.make_async_copy(
                eta.at[:, :, lanes],
                disp.at[0, j, pl.ds(1, levels), pl.ds(0, rows), :],
                load_sem.at[j],
            )
        )
        loads.append(
            pltpu.make_async_copy(
                flow.at[:, :, lanes], mom.at[j, :, pl.ds(0, rows), :], load_sem.at[blocks + j]
            )
        )
    load_res = pltpu.make_async_copy(residual, res_buf, load_sem.at[2 * blocks])
    load_cell = pltpu.make_async_copy(cells.at[own], cell_buf, load_sem.at[2 * blocks + 1])
    load_depth = pltpu.make_async_copy(depth, depth_own, load_sem.at[2 * blocks + 2])
    load_res.start()
    load_cell.start()
    load_depth.start()
    for copy in loads:
        copy.start()

    edge_in[...] = jnp.zeros_like(edge_in)
    if tiles < SLOTS:
        recv[...] = jnp.zeros_like(recv)

    barrier = pltpu.get_barrier_semaphore()
    after = lax.rem(own + 1, tiles)
    before = lax.rem(own + tiles - 1, tiles)

    def greet(tile, window):
        pl.semaphore_signal(
            barrier, inc=1, device_id={"trench": tile, "tblock": window}, device_id_type=MESH
        )

    greet(after, win)
    greet(before, win)

    def greet_tile(i, carry):
        greet(lax.rem(own + i, tiles), win)
        return carry

    lax.fori_loop(2, tiles - 1, greet_tile, 0)

    def greet_window(i, carry):
        greet(own, lax.rem(win + i, windows))
        return carry

    lax.fori_loop(1, windows, greet_window, 0)

    @pl.when(win < reach)
    def _():
        def step(i, carry):
            greet(before, i)
            return carry

        lax.fori_loop(0, windows, step, 0)

    @pl.when(win >= rows - reach)
    def _():
        def step(i, carry):
            greet(after, i)
            return carry

        lax.fori_loop(0, windows, step, 0)

    zero_tile = jnp.zeros((SUB, LANES), f32)
    for j in range(blocks):
        disp[0, j, :, pl.ds(rows, RING - rows), :] = jnp.zeros(
            (levels + 2, RING - rows, LANES), f32
        )
        mom[j, :, pl.ds(rows, RING - rows), :] = jnp.zeros((levels, RING - rows, LANES), f32)
        for s in range(steps):
            for edge in (0, levels + 1):
                disp[s, j, edge] = jnp.zeros((RING, LANES), f32)
    total[pl.ds(windows * part, RING + SUB), :] = jnp.zeros((RING + SUB, LANES), f32)

    load_res.wait()
    load_cell.wait()
    live_count = counts[pl.ds(own, 1), :]
    slot = lax.broadcasted_iota(jnp.int32, (half, tiles), 0)
    pieces = []
    cell_pieces = []
    for h in range(2):
        live = slot + h * half < live_count
        for t in range(steps):
            pieces.append(
                jnp.where(live, res_buf[pl.ds(t * cap + h * half, half), :], f32(0.0))
            )
        cell = cell_buf[pl.ds(h * half, half), :]
        cell_pieces.append((cell % (blocks * LANES)).astype(f32))
        cell_pieces.append((cell // (blocks * LANES)).astype(f32))
        cell_pieces.append(jnp.zeros((2 * half, tiles), f32))
    msg[:, 0, :] = jnp.transpose(jnp.concatenate(pieces, axis=0))
    msg[:, 1, :] = jnp.transpose(jnp.concatenate(cell_pieces, axis=0))
    recv[pl.ds(own, 1)] = msg[pl.ds(own, 1)]

    load_depth.wait()
    pl.semaphore_wait(barrier, (tiles - 1) + (windows - 1) + 2 * reach)

    to_before = pltpu.make_async_remote_copy(
        src_ref=depth_own.at[pl.ds(0, SUB)],
        dst_ref=depth_low,
        send_sem=depth_send.at[0],
        recv_sem=depth_recv.at[0],
        device_id={"trench": before, "tblock": win},
        device_id_type=MESH,
    )
    to_after = pltpu.make_async_remote_copy(
        src_ref=depth_own.at[pl.ds(rows - SUB, SUB)],
        dst_ref=depth_high,
        send_sem=depth_send.at[1],
        recv_sem=depth_recv.at[1],
        device_id={"trench": after, "tblock": win},
        device_id_type=MESH,
    )
    to_before.start()
    to_after.start()

    def send_residual(i, carry):
        owner = lax.rem(own + i, tiles)
        pltpu.make_async_remote_copy(
            src_ref=msg.at[owner],
            dst_ref=recv.at[own],
            send_sem=res_send,
            recv_sem=res_recv,
            device_id={"trench": owner, "tblock": win},
            device_id_type=MESH,
        ).start()
        return carry

    lax.fori_loop(1, tiles, send_residual, 0)

    to_before.wait_recv()
    to_after.wait_recv()
    sub = lax.broadcasted_iota(jnp.int32, (SUB, LANES), 0)
    lane = lax.broadcasted_iota(jnp.int32, (SUB, LANES), 1)
    for j in range(blocks):
        lanes = pl.ds(j * LANES, LANES)
        depth_ring[j, pl.ds(0, rows), :] = depth_own[:, lanes]
        depth_ring[j, pl.ds(rows, SUB), :] = jnp.where(
            sub < reach, depth_low[:, lanes], depth_high[:, lanes]
        )
    for k in range(PHASES):
        ring_row = sub * PHASES + k
        first = jnp.where(own == 0, 0, 1)
        last = jnp.where(own == tiles - 1, 0, 1)
        valid = jnp.where(ring_row < rows, 1, jnp.where(ring_row < rows + reach, last, first))
        for j in range(blocks):
            classes = depth_ring[j, pl.ds(k, SUB, stride=PHASES), :]
            value = jnp.zeros((SUB, LANES), f32)
            for index in range(speed.shape[0]):
                value = jnp.where(classes == index, speed[index], value)
            value = jnp.where(valid == 1, value, f32(0.0))
            coef[0, j, k] = value
            coef[1, j, k] = 4.0 * value + 2.0 * VERT

    for copy in loads:
        copy.wait()

    def load_disp(s, level):
        if s == 0:
            return [
                [disp[0, j, level + 1, pl.ds(k, SUB, stride=PHASES), :] for k in range(PHASES)]
                for j in range(blocks)
            ]
        return [
            [disp[s, j, level + 1, pl.ds(k * SUB, SUB), :] for k in range(PHASES)]
            for j in range(blocks)
        ]

    at_left = lane == 0
    at_right = lane == LANES - 1

    def update(s, level, below, here, above, acc, source=None):
        damp = damping[level]
        weight = profile[level]
        fresh = []
        for k in range(PHASES):
            turned = [pltpu.roll(here[j][k], 1, axis=1) for j in range(blocks)]
            back = [pltpu.roll(here[j][k], LANES - 1, axis=1) for j in range(blocks)]
            for j in range(blocks):
                left = jnp.where(at_left, turned[j - 1] if j > 0 else f32(0.0), turned[j])
                right = jnp.where(
                    at_right, back[j + 1] if j < blocks - 1 else f32(0.0), back[j]
                )
                up = here[j][k - 1] if k > 0 else pltpu.roll(here[j][PHASES - 1], 1, axis=0)
                down = (
                    here[j][k + 1]
                    if k < PHASES - 1
                    else pltpu.roll(here[j][0], SUB - 1, axis=0)
                )
                if s == 0:
                    old = mom[j, level, pl.ds(k, SUB, stride=PHASES), :]
                else:
                    old = mom[j, level, pl.ds(k * SUB, SUB), :]
                new = (
                    damp * old
                    + coef[0, j, k] * ((left + right) + (up + down))
                    + VERT * (below[j][k] + above[j][k])
                    - coef[1, j, k] * here[j][k]
                )
                if source is not None:
                    new = new + inject[
                        pl.ds((source * PHASES + k) * SUB, SUB), pl.ds(j * LANES, LANES)
                    ]
                fresh.append((j, k, new))
        for j, k, new in fresh:
            if s < steps - 1:
                mom[j, level, pl.ds(k * SUB, SUB), :] = new
                disp[s + 1, j, level + 1, pl.ds(k * SUB, SUB), :] = here[j][k] + new
        acc = list(acc)
        for j, k, new in fresh:
            acc[j * PHASES + k] = acc[j * PHASES + k] + weight * new
        return acc

    def sweep(s, base, count, acc, bottom):
        below = load_disp(s, base - 1)
        here = load_disp(s, base)
        for i in range(count):
            above = load_disp(s, base + i + 1)
            source = steps - 1 - s if bottom and i == count - 1 else None
            acc = update(s, base + i, below, here, above, acc, source)
            below, here = here, above
        return acc

    for s in range(steps):
        ready = levels - 2 - s
        size = divisor(ready, 13)

        def chunk(i, acc, s=s, size=size):
            return tuple(sweep(s, i * size, size, acc, False))

        acc = lax.fori_loop(0, ready // size, chunk, (zero_tile,) * (blocks * PHASES))
        for n, value in enumerate(acc):
            acc_ref[s, n] = value

    wait_all = pltpu.make_async_copy(
        recv.at[pl.ds(0, tiles - 1)], recv.at[pl.ds(0, tiles - 1)], res_recv
    )
    wait_all.wait()
    values = recv[:, 0, :]
    places = recv[:, 1, :]
    values = jnp.transpose(
        jnp.concatenate([values, pltpu.roll(values, LANES // 2, axis=1)], axis=0)
    )
    places = jnp.transpose(
        jnp.concatenate([places, pltpu.roll(places, LANES // 2, axis=1)], axis=0)
    )
    cols[...] = jnp.concatenate([values[: steps * half], places[: 2 * half]], axis=0)
    ring_rows = [(sub * PHASES + k).astype(f32) for k in range(PHASES)]
    columns = lax.broadcasted_iota(jnp.int32, (blocks * LANES, LANES), 0).astype(f32)

    def expand(i, carry):
        lanes = pl.ds(pl.multiple_of(i * LANES, LANES), LANES)
        col = cols[pl.ds(steps * half + i, 1), :]
        row = cols[pl.ds(steps * half + half + i, 1), :]
        match = [row == ring_rows[k] for k in range(PHASES)]
        high, low = [], []
        for t in range(steps):
            value = cols[pl.ds(t * half + i, 1), :]
            coarse = value.astype(jnp.bfloat16).astype(f32)
            fine = value - coarse
            for k in range(PHASES):
                high.append(jnp.where(match[k], coarse, f32(0.0)))
                low.append(jnp.where(match[k], fine, f32(0.0)))
        onehot_row[:, lanes] = jnp.concatenate(high + low, axis=0).astype(jnp.bfloat16)
        onehot_col[:, lanes] = jnp.where(columns == col, f32(1.0), f32(0.0)).astype(jnp.bfloat16)
        return carry

    lax.fori_loop(0, half, expand, 0, unroll=2)
    product = lax.dot_general(
        onehot_row[...],
        onehot_col[...],
        (((1,), (1,)), ((), ())),
        preferred_element_type=f32,
    )
    inject[...] = product[: steps * RING] + product[steps * RING :]

    scale = f32(1.0 / math.sqrt(levels))
    for s in range(steps):
        base = levels - 2 - s
        acc = [acc_ref[s, n] for n in range(blocks * PHASES)]
        acc = sweep(s, base, levels - base, acc, True)
        t = steps - 1 - s
        for j in range(blocks):
            for k in range(PHASES):
                send_rows[pl.ds(k * part + t * blocks + j, SUB, stride=PHASES * part), :] = (
                    acc[j * PHASES + k] * scale
                )

    slot_rows = pl.ds(pl.multiple_of(win * part, part), part)
    edge_copies = []
    for i in range(reach):
        size = part if i < reach // 2 else part // 2
        slot_part = pl.ds(pl.multiple_of(win * part, part), size)
        for ring_row, tile, target in (
            (rows + i, after, i),
            (RING - 1 - i, before, rows - 1 - i),
        ):
            edge_copies.append(
                pltpu.make_async_remote_copy(
                    src_ref=send_rows.at[pl.ds(ring_row * part, size)],
                    dst_ref=edge_in.at[slot_part],
                    send_sem=edge_send.at[len(edge_copies)],
                    recv_sem=edge_recv,
                    device_id={"trench": tile, "tblock": target},
                    device_id_type=MESH,
                )
            )

    def send_row(i, carry):
        target = lax.rem(win + i, windows)
        pltpu.make_async_remote_copy(
            src_ref=send_rows.at[pl.ds(pl.multiple_of(target * part, part), part)],
            dst_ref=rows_in.at[slot_rows],
            send_sem=row_send,
            recv_sem=row_recv,
            device_id={"trench": own, "tblock": target},
            device_id_type=MESH,
        ).start()
        return carry

    lax.fori_loop(1, windows, send_row, 0)
    for copy in edge_copies:
        copy.start()
    rows_in[slot_rows, :] = send_rows[slot_rows, :]

    pltpu.make_async_copy(
        rows_in.at[pl.ds(0, (windows - 1) * part)],
        rows_in.at[pl.ds(0, (windows - 1) * part)],
        row_recv,
    ).wait()

    @pl.when((win < reach // 2) | (win >= rows - reach // 2))
    def _():
        pltpu.make_async_copy(edge_in, edge_in, edge_recv).wait()

    @pl.when(
        ((win >= reach // 2) & (win < reach))
        | ((win < rows - reach // 2) & (win >= rows - reach))
    )
    def _():
        whole = edge_in.at[pl.ds(0, windows * part // 2)]
        pltpu.make_async_copy(whole, whole, edge_recv).wait()

    length = windows * part
    total[pl.ds(0, length), :] = rows_in[...] + edge_in[...]
    result = band[0] * total[pl.ds(0, length), :]
    for offset in range(1, band.shape[0]):
        result = result + band[offset] * total[pl.ds(offset * blocks, length), :]
    out[...] = result

    to_before.wait_send()
    to_after.wait_send()
    pltpu.make_async_copy(
        msg.at[pl.ds(0, tiles - 1)], msg.at[pl.ds(0, tiles - 1)], res_send
    ).wait()
    pltpu.make_async_copy(
        send_rows.at[pl.ds(0, (windows - 1) * part)],
        send_rows.at[pl.ds(0, (windows - 1) * part)],
        row_send,
    ).wait()
    for copy in edge_copies:
        copy.wait_send()


def body(
    tiles,
    windows,
    adjoint_eta,
    adjoint_flow,
    residual,
    sensor_cell,
    sensor_count,
    depth_class,
    speed_table,
    damping,
    profile,
    band_weight,
):
    levels, rows, across = adjoint_eta.shape[1:]
    steps, cap = residual.shape[3:]
    blocks = across // LANES
    part = steps * blocks
    length = windows * part
    f32, i32 = jnp.float32, jnp.int32
    by_owner = jnp.transpose(residual[0, 0], (1, 2, 0)).reshape(steps * cap, tiles)
    cells = jnp.transpose(sensor_cell, (0, 2, 1))
    hbm = pl.BlockSpec(memory_space=pltpu.HBM)
    vmem = pl.BlockSpec(memory_space=pltpu.VMEM)
    smem = pl.BlockSpec(memory_space=pltpu.SMEM)
    dma = pltpu.SemaphoreType.DMA
    result = pl.pallas_call(
        functools.partial(kernel, (tiles, windows, levels, rows, blocks, steps, cap)),
        out_shape=jax.ShapeDtypeStruct((length, LANES), f32),
        in_specs=[hbm, hbm, hbm, hbm, vmem, hbm, smem, smem, smem, smem],
        out_specs=vmem,
        scratch_shapes=[
            pltpu.VMEM((steps, blocks, levels + 2, RING, LANES), f32),
            pltpu.VMEM((blocks, levels, RING, LANES), f32),
            pltpu.VMEM((steps * cap, tiles), f32),
            pltpu.VMEM((cap, tiles), i32),
            pltpu.VMEM((rows, across), i32),
            pltpu.VMEM((SUB, across), i32),
            pltpu.VMEM((SUB, across), i32),
            pltpu.VMEM((blocks, RING, LANES), i32),
            pltpu.VMEM((2, blocks, PHASES, SUB, LANES), f32),
            pltpu.VMEM((tiles, 2, LANES), f32),
            pltpu.VMEM((SLOTS, 2, LANES), f32),
            pltpu.VMEM((2 * steps * RING, SLOTS * cap), jnp.bfloat16),
            pltpu.VMEM((across, SLOTS * cap), jnp.bfloat16),
            pltpu.VMEM((steps * cap // 2 + cap, LANES), f32),
            pltpu.VMEM((steps * RING, across), f32),
            pltpu.VMEM((steps, blocks * PHASES, SUB, LANES), f32),
            pltpu.VMEM((RING * part, LANES), f32),
            pltpu.VMEM((length, LANES), f32),
            pltpu.VMEM((length, LANES), f32),
            pltpu.VMEM((length + RING + SUB, LANES), f32),
            dma((2 * blocks + 3,)),
            dma((2,)),
            dma((2,)),
            dma,
            dma,
            dma,
            dma,
            dma((2 * steps,)),
            dma,
        ],
        compiler_params=pltpu.CompilerParams(
            collective_id=0, has_side_effects=True, vmem_limit_bytes=56 << 20
        ),
        name="adjoint",
    )(
        adjoint_eta[0],
        adjoint_flow[0],
        by_owner,
        cells,
        sensor_count,
        depth_class,
        speed_table,
        damping,
        profile,
        band_weight,
    )
    return result.reshape(windows * steps, 1, across)


def solution(mesh):
    in_specs = (
        P("tblock", None, "trench", None),
        P("tblock", None, "trench", None),
        P("tblock", "trench", None, None, None),
        P(),
        P(),
        P("trench", None),
        P(),
        P(),
        P(),
        P(),
    )
    out_specs = P(None, ("trench", "tblock"), None)
    sizes = mesh.shape
    return jax.shard_map(
        functools.partial(body, sizes["trench"], sizes["tblock"]),
        mesh=mesh,
        in_specs=in_specs,
        out_specs=out_specs,
        check_vma=False,
    )
```

time: 158 us -> 47.6 us (0.30)
  the two profiles are of different devices: /device:TPU:64 before, /device:TPU:1 now
where the time goes in v1:
time: 47.6 us; the launch traced here: 47.3 us
  Pallas kernels  45.8 us (96%)
  local copies, waits for them, and re-layouts  1.57 us (3%)
    pallas_call x1, Pallas kernels, body(): pl.pallas_call(functools.partial(kernel, (tiles, windows, levels, rows, b...  45.8 us
    unnamed x1, local copies, waits for them, and re-layouts  1.57 us

profile of v1, /device:TPU:1, one launch (start us, length us, event | category | flops | bytes accessed | tf_op | source)
XLA Modules:
  0.0 47.3 jit_solution(13960766776034324940)
XLA Ops:
  0.0 45.8 %adjoint.1 = f32[256,128]{1,0:T(8,128)} custom-call(f32[30,16,512]{2,1,0:T(8,128)} %bitcast.10, f32[30,16,512]{2,1,0:T(8,128)} %bitcast.11, f32[128,64]{1,0:T(8,128)} %bitcast.13, s32[64,32,64]{2,1,0:T(8,128)} %bitcast.9, s32[64,64]{1,0:T(8,128)} %counts.1, s32[16,512]{1,0:T(8,128)} %depth.1, f32[8]{0:T(128)} %speed.1, f32[30]{0:T(128)} %damping.1, ...), custom_call_target="tpu_custom_call" | custom-call | tf_op jit(solution)/shard_map/adjoint/pallas_call | solution.py:470
  45.8 1.6 %copy.13 = f32[64,1,512]{2,1,0:T(1,128)} copy(f32[64,1,512]{2,1,0:T(1,128)} %bitcast.12) | data formatting | bytes 262144

commit v2 on v1

v2 whole, which is shorter than its diff:
```python
import functools
import math

import jax
import jax.numpy as jnp
from jax import lax
from jax.experimental import pallas as pl
from jax.experimental.pallas import tpu as pltpu
from jax.sharding import PartitionSpec as P

VERT = 0.2
MESH = pl.DeviceIdType.MESH
LANES = 128
SUB = 8
PHASES = 3
RING = PHASES * SUB
SLOTS = 64
TAIL = 32


def kernel(
    cfg,
    eta,
    flow,
    residual,
    cells,
    counts,
    depth,
    speed,
    damping,
    profile,
    total,
    disp,
    mom,
    level_rows,
    weights,
    gammas,
    fields,
    res_buf,
    cell_buf,
    depth_own,
    depth_low,
    depth_high,
    depth_ring,
    celerity,
    msg,
    recv,
    onehot_row,
    onehot_col,
    places,
    cols,
    inject,
    send_rows,
    rows_in,
    edge_in,
    load_sem,
    depth_send,
    depth_recv,
    res_send,
    res_recv,
    row_send,
    row_recv,
    edge_send,
    edge_recv,
    half_in,
    beside_in,
):
    tiles, windows, levels, rows, blocks, steps, cap = cfg
    own = lax.axis_index("trench")
    win = lax.axis_index("tblock")
    f32 = jnp.float32
    reach = steps
    part = steps * blocks
    half = cap // 2
    side = windows // 2

    load_res = pltpu.make_async_copy(residual, res_buf, load_sem.at[0])
    load_cell = pltpu.make_async_copy(cells, cell_buf, load_sem.at[1])
    load_depth = pltpu.make_async_copy(depth, depth_own, load_sem.at[2])
    load_eta = pltpu.make_async_copy(eta, disp, load_sem.at[3])
    load_flow = pltpu.make_async_copy(flow, mom, load_sem.at[4])
    load_res.start()
    load_depth.start()
    load_eta.start()
    load_flow.start()
    load_cell.start()

    edge_in[...] = jnp.zeros_like(edge_in)
    if tiles < SLOTS:
        recv[...] = jnp.zeros_like(recv)

    barrier = pltpu.get_barrier_semaphore()
    after = lax.rem(own + 1, tiles)
    before = lax.rem(own + tiles - 1, tiles)

    def greet(tile, window):
        pl.semaphore_signal(
            barrier, inc=1, device_id={"trench": tile, "tblock": window}, device_id_type=MESH
        )

    def other_tile(i):
        away = lax.div(i + 1, 2)
        return lax.rem(own + tiles // 2 + jnp.where(lax.rem(i, 2) == 1, away, tiles - away), tiles)

    def greet_tile(i, carry):
        greet(other_tile(i), win)
        return carry

    lax.fori_loop(0, tiles - 1, greet_tile, 0)

    my_side = lax.div(win, side)
    my_place = lax.rem(win, side)
    twin = lax.rem(win + side, windows)

    def greet_window(i, carry):
        greet(own, my_side * side + lax.rem(my_place + i, side))
        return carry

    lax.fori_loop(1, side, greet_window, 0)
    greet(own, twin)

    def tell(semaphore, tile, window):
        pl.semaphore_signal(
            semaphore, inc=1, device_id={"trench": tile, "tblock": window}, device_id_type=MESH
        )

    load_res.wait()
    live_count = counts[pl.ds(own, 1), :]
    slot = lax.broadcasted_iota(jnp.int32, (half, tiles), 0)
    pieces = []
    for h in range(2):
        live = slot + h * half < live_count
        for t in range(steps):
            pieces.append(
                jnp.where(live, res_buf[pl.ds(t * cap + h * half, half), :], f32(0.0))
            )
    msg[:, 0, :] = jnp.transpose(jnp.concatenate(pieces, axis=0))
    recv[pl.ds(own, 1)] = msg[pl.ds(own, 1)]
    load_depth.wait()

    to_before = pltpu.make_async_remote_copy(
        src_ref=depth_own.at[pl.ds(0, SUB)],
        dst_ref=depth_low,
        send_sem=depth_send.at[0],
        recv_sem=depth_recv.at[0],
        device_id={"trench": before, "tblock": win},
        device_id_type=MESH,
    )
    to_after = pltpu.make_async_remote_copy(
        src_ref=depth_own.at[pl.ds(rows - SUB, SUB)],
        dst_ref=depth_high,
        send_sem=depth_send.at[1],
        recv_sem=depth_recv.at[1],
        device_id={"trench": after, "tblock": win},
        device_id_type=MESH,
    )

    def send_residual(i, carry):
        owner = other_tile(i)
        pltpu.make_async_remote_copy(
            src_ref=msg.at[owner],
            dst_ref=recv.at[own],
            send_sem=res_send,
            recv_sem=res_recv,
            device_id={"trench": owner, "tblock": win},
            device_id_type=MESH,
        ).start()
        return carry

    def exchange():
        pl.semaphore_wait(barrier, (tiles - 1) + (side - 1) + 1)
        to_before.start()
        to_after.start()
        tell(half_in, own, twin)
        lax.fori_loop(0, tiles - 1, send_residual, 0)

    hurry = (win >= side) & (lax.rem(own, 8) >= min(tiles, 8) // 2)

    @pl.when(hurry)
    def _():
        exchange()

    padded = level_rows.shape[1]
    level_rows[...] = jnp.zeros_like(level_rows)
    for level in range(levels):
        level_rows[0, pl.ds(level, 1), :] = jnp.full((1, LANES), profile[level], f32)
        level_rows[1, pl.ds(level, 1), :] = jnp.full((1, LANES), damping[level], f32)
    weight = level_rows[0]
    damp = level_rows[1]
    inside = lax.broadcasted_iota(jnp.int32, (padded, LANES), 0) < levels

    def vertical(x):
        pair = pltpu.roll(x, 1, axis=0) + pltpu.roll(x, padded - 1, axis=0)
        return jnp.where(inside, VERT * (pair - 2.0 * x), f32(0.0))

    def add(x, y):
        return [
            x[i] + y[i] if i < len(x) and i < len(y) else (x[i] if i < len(x) else y[i])
            for i in range(max(len(x), len(y)))
        ]

    alpha, beta = [weight], []
    sigma = [weight]
    alphas, betas, sigmas = [], [], []
    for _ in range(steps):
        sigmas.append(sigma)
        alpha = [damp * x for x in sigma]
        raised = [jnp.zeros_like(weight)] + sigma
        beta = add(add(beta, [vertical(x) for x in sigma]), raised)
        sigma = add(alpha, beta)
        alphas.append(alpha)
        betas.append(beta)
    slots = [(s, k) for s in range(1, steps + 1) for k in range(s)]
    place = {key: n for n, key in enumerate(slots)}
    on_disp, on_mom = [], []
    count = 0
    for s, k in slots:
        weights[count] = betas[s - 1][k]
        on_disp.append((count, place[s, k]))
        count += 1
        if k < s - 1:
            weights[count] = alphas[s - 1][k]
            on_mom.append((count, place[s, k]))
            count += 1
    weights[count] = weight
    on_disp.append((count, len(slots)))
    weights[count + 1] = damp * weight
    on_mom.append((count + 1, len(slots) + 1))
    gamma_place = {}
    for j in range(steps):
        for k in range(j + 1):
            n = len(gamma_place)
            gamma_place[j, k] = n
            gammas[pl.ds(n, 1), :] = sigmas[j][k][levels - 1 : levels]

    load_eta.wait()
    load_flow.wait()
    n_acc = len(slots) + 2
    zero_tile = jnp.zeros((SUB, LANES), f32)
    for j in range(blocks):
        for n in range(len(slots) + 1):
            fields[n, j, pl.ds(rows, RING - rows), :] = jnp.zeros((RING - rows, LANES), f32)
    for r in range(rows // SUB):
        tile_rows = pl.ds(r * SUB, SUB)

        def contract(level, acc, tile_rows=tile_rows):
            acc = list(acc)
            d = [disp[level, tile_rows, pl.ds(j * LANES, LANES)] for j in range(blocks)]
            m = [mom[level, tile_rows, pl.ds(j * LANES, LANES)] for j in range(blocks)]
            for source, table in ((d, on_disp), (m, on_mom)):
                for row, target in table:
                    w = jnp.broadcast_to(weights[row, pl.ds(level, 1), :], (SUB, LANES))
                    for j in range(blocks):
                        n = target * blocks + j
                        acc[n] = acc[n] + w * source[j]
            return tuple(acc)

        acc = lax.fori_loop(0, levels, contract, (zero_tile,) * (n_acc * blocks), unroll=2)
        for j in range(blocks):
            shared = acc[(len(slots) + 1) * blocks + j]
            for s, k in slots:
                value = acc[place[s, k] * blocks + j]
                fields[place[s, k], j, tile_rows, :] = value + shared if k == s - 1 else value
            fields[len(slots), j, tile_rows, :] = acc[len(slots) * blocks + j]

    load_cell.wait()
    pick = jnp.where(
        lax.broadcasted_iota(jnp.int32, (SUB, tiles), 1) == own, f32(1.0), f32(0.0)
    ).astype(jnp.bfloat16)
    shift = (blocks * LANES).bit_length() - 1
    columns = lax.broadcasted_iota(jnp.int32, (blocks * LANES, LANES), 0).astype(f32)
    for i in range(half):
        sources = []
        for h in range(2):
            sources.append(cell_buf[:, h * half + i, :])
            if tiles < SLOTS:
                sources.append(jnp.zeros((SLOTS - tiles, tiles), jnp.int32))
        cell = jnp.concatenate(sources, axis=0)
        column = cell & (blocks * LANES - 1)
        digits = [cell >> shift, column >> 7, column & (LANES - 1)]
        digits = jnp.concatenate([x.astype(f32) for x in digits], axis=0).astype(jnp.bfloat16)
        found = lax.dot_general(
            pick, digits, (((1,), (1,)), ((), ())), preferred_element_type=f32
        )
        places[pl.ds(half + i, 1), :] = found[:1, :LANES]
        places[pl.ds(i, 1), :] = found[:1, LANES : 2 * LANES] * LANES + found[:1, 2 * LANES :]

    def expand_columns(i, carry):
        lanes = pl.ds(pl.multiple_of(i * LANES, LANES), LANES)
        match = columns == places[pl.ds(i, 1), :]
        onehot_col[:, lanes] = jnp.where(match, f32(1.0), f32(0.0)).astype(jnp.bfloat16)
        return carry

    lax.fori_loop(0, half, expand_columns, 0, unroll=2)

    @pl.when(jnp.logical_not(hurry))
    def _():
        exchange()

    to_before.wait_recv()
    to_after.wait_recv()
    sub = lax.broadcasted_iota(jnp.int32, (SUB, LANES), 0)
    lane = lax.broadcasted_iota(jnp.int32, (SUB, LANES), 1)
    for j in range(blocks):
        lanes = pl.ds(j * LANES, LANES)
        depth_ring[j, pl.ds(0, rows), :] = depth_own[:, lanes]
        depth_ring[j, pl.ds(rows, SUB), :] = jnp.where(
            sub < reach, depth_low[:, lanes], depth_high[:, lanes]
        )
    for k in range(PHASES):
        ring_row = sub * PHASES + k
        first = jnp.where(own == 0, 0, 1)
        last = jnp.where(own == tiles - 1, 0, 1)
        valid = jnp.where(ring_row < rows, 1, jnp.where(ring_row < rows + reach, last, first))
        for j in range(blocks):
            classes = depth_ring[j, pl.ds(k, SUB, stride=PHASES), :]
            value = jnp.zeros((SUB, LANES), f32)
            for index in range(speed.shape[0]):
                value = jnp.where(classes == index, speed[index], value)
            celerity[j, k] = jnp.where(valid == 1, value, f32(0.0))

    pl.semaphore_wait(half_in, 1)
    tell(beside_in, before, win)
    tell(beside_in, after, win)

    pltpu.make_async_copy(
        recv.at[pl.ds(0, tiles - 1)], recv.at[pl.ds(0, tiles - 1)], res_recv
    ).wait()
    values = recv[:, 0, :]
    values = jnp.transpose(
        jnp.concatenate([values, pltpu.roll(values, LANES // 2, axis=1)], axis=0)
    )
    cols[...] = values[: steps * half]
    ring_rows = [(sub * PHASES + k).astype(f32) for k in range(PHASES)]

    def expand(i, carry):
        lanes = pl.ds(pl.multiple_of(i * LANES, LANES), LANES)
        row = places[pl.ds(half + i, 1), :]
        match = [row == ring_rows[k] for k in range(PHASES)]
        high, low = [], []
        for t in range(steps):
            value = cols[pl.ds(t * half + i, 1), :]
            coarse = value.astype(jnp.bfloat16).astype(f32)
            fine = value - coarse
            for k in range(PHASES):
                high.append(jnp.where(match[k], coarse, f32(0.0)))
                low.append(jnp.where(match[k], fine, f32(0.0)))
        onehot_row[:, lanes] = jnp.concatenate(high + low, axis=0).astype(jnp.bfloat16)
        return carry

    lax.fori_loop(0, half, expand, 0, unroll=2)
    product = lax.dot_general(
        onehot_row[...],
        onehot_col[...],
        (((1,), (1,)), ((), ())),
        preferred_element_type=f32,
    )
    inject[...] = product[: steps * RING] + product[steps * RING :]

    at_left = lane == 0
    at_right = lane == LANES - 1
    scale = f32(1.0 / math.sqrt(levels))

    def laplace(x):
        result = [[None] * PHASES for _ in range(blocks)]
        for k in range(PHASES):
            turned = [pltpu.roll(x[j][k], 1, axis=1) for j in range(blocks)]
            back = [pltpu.roll(x[j][k], LANES - 1, axis=1) for j in range(blocks)]
            for j in range(blocks):
                left = jnp.where(at_left, turned[j - 1] if j > 0 else f32(0.0), turned[j])
                right = jnp.where(
                    at_right, back[j + 1] if j < blocks - 1 else f32(0.0), back[j]
                )
                up = x[j][k - 1] if k > 0 else pltpu.roll(x[j][PHASES - 1], 1, axis=0)
                down = x[j][k + 1] if k < PHASES - 1 else pltpu.roll(x[j][0], SUB - 1, axis=0)
                around = (left + right) + (up + down)
                result[j][k] = celerity[j, k] * (around - 4.0 * x[j][k])
        return result

    def field(n):
        return [
            [fields[n, j, pl.ds(k, SUB, stride=PHASES), :] for k in range(PHASES)]
            for j in range(blocks)
        ]

    def plus(x, y):
        return [[x[j][k] + y[j][k] for k in range(PHASES)] for j in range(blocks)]

    def source(s, power):
        value = field(place[s, power])
        for n in range(1, s - power + 1):
            g = gammas[pl.ds(gamma_place[s - n, power], 1), :]
            t = steps - n
            for j in range(blocks):
                for k in range(PHASES):
                    value[j][k] = value[j][k] + g * inject[
                        pl.ds((t * PHASES + k) * SUB, SUB), pl.ds(j * LANES, LANES)
                    ]
        return value

    top = laplace(field(len(slots)))
    for s in range(1, steps + 1):
        value = plus(source(s, s - 1), top)
        for power in range(s - 2, -1, -1):
            value = plus(source(s, power), laplace(value))
        t = steps - s
        for j in range(blocks):
            for k in range(PHASES):
                send_rows[pl.ds(k * part + t * blocks + j, SUB, stride=PHASES * part), :] = (
                    value[j][k] * scale
                )

    slot_rows = pl.ds(pl.multiple_of(win * part, part), part)
    edge_copies = []
    for i in range(reach):
        size = part if i < reach // 2 else part // 2
        slot_part = pl.ds(pl.multiple_of(win * part, part), size)
        for ring_row, tile, target in (
            (rows + i, after, i),
            (RING - 1 - i, before, rows - 1 - i),
        ):
            edge_copies.append(
                pltpu.make_async_remote_copy(
                    src_ref=send_rows.at[pl.ds(ring_row * part, size)],
                    dst_ref=edge_in.at[slot_part],
                    send_sem=edge_send.at[len(edge_copies)],
                    recv_sem=edge_recv,
                    device_id={"trench": tile, "tblock": target},
                    device_id_type=MESH,
                )
            )
    pl.semaphore_wait(beside_in, 2)
    for copy in edge_copies:
        copy.start()

    def send_row(target):
        pltpu.make_async_remote_copy(
            src_ref=send_rows.at[pl.ds(pl.multiple_of(target * part, part), part)],
            dst_ref=rows_in.at[slot_rows],
            send_sem=row_send,
            recv_sem=row_recv,
            device_id={"trench": own, "tblock": target},
            device_id_type=MESH,
        ).start()

    def send_far(i, carry):
        send_row((1 - my_side) * side + lax.rem(my_place + side // 2 + i, side))
        return carry

    def send_near(i, carry):
        send_row(my_side * side + lax.rem(my_place + i, side))
        return carry

    lax.fori_loop(0, side, send_far, 0)
    lax.fori_loop(1, side, send_near, 0)
    rows_in[slot_rows, :] = send_rows[slot_rows, :]

    pltpu.make_async_copy(
        rows_in.at[pl.ds(0, (windows - 1) * part)],
        rows_in.at[pl.ds(0, (windows - 1) * part)],
        row_recv,
    ).wait()

    @pl.when((win < reach // 2) | (win >= rows - reach // 2))
    def _():
        pltpu.make_async_copy(edge_in, edge_in, edge_recv).wait()

    @pl.when(
        ((win >= reach // 2) & (win < reach))
        | ((win < rows - reach // 2) & (win >= rows - reach))
    )
    def _():
        whole = edge_in.at[pl.ds(0, windows * part // 2)]
        pltpu.make_async_copy(whole, whole, edge_recv).wait()

    length = windows * part
    total[pl.ds(0, length), :] = rows_in[...] + edge_in[...]
    total[pl.ds(length, TAIL), :] = jnp.zeros((TAIL, LANES), f32)

    to_before.wait_send()
    to_after.wait_send()
    pltpu.make_async_copy(
        msg.at[pl.ds(0, tiles - 1)], msg.at[pl.ds(0, tiles - 1)], res_send
    ).wait()
    pltpu.make_async_copy(
        send_rows.at[pl.ds(0, (windows - 1) * part)],
        send_rows.at[pl.ds(0, (windows - 1) * part)],
        row_send,
    ).wait()
    for copy in edge_copies:
        copy.wait_send()


def prior(blocks, length, total, band, out):
    result = band[0] * total[pl.ds(0, length), :]
    for offset in range(1, band.shape[0]):
        result = result + band[offset] * total[pl.ds(offset * blocks, length), :]
    out[...] = result


def body(
    tiles,
    windows,
    adjoint_eta,
    adjoint_flow,
    residual,
    sensor_cell,
    sensor_count,
    depth_class,
    speed_table,
    damping,
    profile,
    band_weight,
):
    levels, rows, across = adjoint_eta.shape[1:]
    steps, cap = residual.shape[3:]
    blocks = across // LANES
    part = steps * blocks
    length = windows * part
    f32, i32 = jnp.float32, jnp.int32
    padded = (levels // SUB + 1) * SUB
    pairs = steps * (steps + 1) // 2
    by_owner = jnp.transpose(residual[0, 0], (1, 2, 0)).reshape(steps * cap, tiles)
    cells = jnp.transpose(sensor_cell, (0, 2, 1))
    hbm = pl.BlockSpec(memory_space=pltpu.HBM)
    vmem = pl.BlockSpec(memory_space=pltpu.VMEM)
    smem = pl.BlockSpec(memory_space=pltpu.SMEM)
    dma = pltpu.SemaphoreType.DMA
    total = pl.pallas_call(
        functools.partial(kernel, (tiles, windows, levels, rows, blocks, steps, cap)),
        out_shape=jax.ShapeDtypeStruct((length + TAIL, LANES), f32),
        in_specs=[hbm, hbm, hbm, hbm, vmem, hbm, smem, smem, smem],
        out_specs=vmem,
        scratch_shapes=[
            pltpu.VMEM((levels, rows, across), f32),
            pltpu.VMEM((levels, rows, across), f32),
            pltpu.VMEM((2, padded, LANES), f32),
            pltpu.VMEM((pairs + (steps - 1) * steps // 2 + 2, padded, LANES), f32),
            pltpu.VMEM((2 * SUB, LANES), f32),
            pltpu.VMEM((pairs + 1, blocks, RING, LANES), f32),
            pltpu.VMEM((steps * cap, tiles), f32),
            pltpu.VMEM((tiles, cap, tiles), i32),
            pltpu.VMEM((rows, across), i32),
            pltpu.VMEM((SUB, across), i32),
            pltpu.VMEM((SUB, across), i32),
            pltpu.VMEM((blocks, RING, LANES), i32),
            pltpu.VMEM((blocks, PHASES, SUB, LANES), f32),
            pltpu.VMEM((tiles, 1, LANES), f32),
            pltpu.VMEM((SLOTS, 1, LANES), f32),
            pltpu.VMEM((2 * steps * RING, SLOTS * cap), jnp.bfloat16),
            pltpu.VMEM((across, SLOTS * cap), jnp.bfloat16),
            pltpu.VMEM((cap, LANES), f32),
            pltpu.VMEM((steps * cap // 2, LANES), f32),
            pltpu.VMEM((steps * RING, across), f32),
            pltpu.VMEM((RING * part, LANES), f32),
            pltpu.VMEM((length, LANES), f32),
            pltpu.VMEM((length, LANES), f32),
            dma((5,)),
            dma((2,)),
            dma((2,)),
            dma,
            dma,
            dma,
            dma,
            dma((2 * steps,)),
            dma,
            pltpu.SemaphoreType.REGULAR,
            pltpu.SemaphoreType.REGULAR,
        ],
        compiler_params=pltpu.CompilerParams(
            collective_id=0, has_side_effects=True, vmem_limit_bytes=56 << 20
        ),
        name="adjoint",
    )(
        adjoint_eta[0],
        adjoint_flow[0],
        by_owner,
        cells,
        sensor_count,
        depth_class,
        speed_table,
        damping,
        profile,
    )
    result = pl.pallas_call(
        functools.partial(prior, blocks, length),
        out_shape=jax.ShapeDtypeStruct((length, LANES), f32),
        in_specs=[vmem, smem],
        out_specs=vmem,
        name="prior",
    )(total, band_weight)
    return result.reshape(windows * steps, 1, across)


def solution(mesh):
    in_specs = (
        P("tblock", None, "trench", None),
        P("tblock", None, "trench", None),
        P("tblock", "trench", None, None, None),
        P(),
        P(),
        P("trench", None),
        P(),
        P(),
        P(),
        P(),
    )
    out_specs = P(None, ("trench", "tblock"), None)
    sizes = mesh.shape
    return jax.shard_map(
        functools.partial(body, sizes["trench"], sizes["tblock"]),
        mesh=mesh,
        in_specs=in_specs,
        out_specs=out_specs,
        check_vma=False,
    )
```

time: 47.6 us -> 43.9 us (0.922)
  Pallas kernels: 45.8 us -> 43.7 us
  local copies, waits for them, and re-layouts: 1.57 us -> 0 us
    pallas_call x1, Pallas kernels: 45.8 us -> 42 us  [body(): pl.pallas_call(functools.partial(kernel, (tiles, windows, levels, rows, b...]
    pallas_call x0 -> x1, Pallas kernels: none -> 1.65 us  [body(): pl.pallas_call(functools.partial(prior, blocks, length), out_shape=jax.Sh...]
    unnamed x1 -> x0, local copies, waits for them, and re-layouts: 1.57 us -> none
where the time goes in v2:
time: 43.9 us; the launch traced here: 43.7 us
  Pallas kernels  43.7 us (100%)
    pallas_call x1, Pallas kernels, body(): pl.pallas_call(functools.partial(kernel, (tiles, windows, levels, rows, b...  42 us
    pallas_call x1, Pallas kernels, body(): pl.pallas_call(functools.partial(prior, blocks, length), out_shape=jax.Sh...  1.65 us

profile of v2, /device:TPU:1, one launch (start us, length us, event | category | flops | bytes accessed | tf_op | source)
XLA Modules:
  0.0 43.7 jit_solution(856111598536268534)
XLA Ops:
  0.0 42.0 %adjoint.1.total = f32[288,128]{1,0:T(8,128)} custom-call(f32[30,16,512]{2,1,0:T(8,128)} %bitcast.10, f32[30,16,512]{2,1,0:T(8,128)} %bitcast.11, f32[128,64]{1,0:T(8,128)} %bitcast.12, s32[64,32,64]{2,1,0:T(8,128)} %bitcast.9, s32[64,64]{1,0:T(8,128)} %counts.1, s32[16,512]{1,0:T(8,128)} %depth.1, f32[8]{0:T(128)} %speed.1, f32[30]{0:T(128)} %damping.1, ...), custom_call_target="tpu_custom_call" | custom-call | tf_op jit(solution)/shard_map/adjoint/pallas_call | solution.py:529
  42.0 1.6 %prior.1 = f32[256,128]{1,0:T(8,128)} custom-call(f32[288,128]{1,0:T(8,128)} %adjoint.1.total, f32[8]{0:T(128)} %band.1), custom_call_target="tpu_custom_call" | custom-call | tf_op jit(solution)/shard_map/prior/pallas_call | solution.py:585

commit v3 on v2

--- a/solution.py
+++ b/solution.py
@@ -24,12 +24,16 @@
     flow,
     residual,
     cells,
+    counts_hbm,
+    depth,
+    speed_hbm,
+    damping_hbm,
+    profile_hbm,
+    total,
     counts,
-    depth,
     speed,
     damping,
     profile,
-    total,
     disp,
     mom,
     level_rows,
@@ -50,6 +54,7 @@
     places,
     cols,
     inject,
+    from_state,
     send_rows,
     rows_in,
     edge_in,
@@ -79,8 +84,17 @@
     load_depth = pltpu.make_async_copy(depth, depth_own, load_sem.at[2])
     load_eta = pltpu.make_async_copy(eta, disp, load_sem.at[3])
     load_flow = pltpu.make_async_copy(flow, mom, load_sem.at[4])
+    load_counts = pltpu.make_async_copy(counts_hbm, counts, load_sem.at[5])
+    small = [
+        pltpu.make_async_copy(speed_hbm, speed, load_sem.at[6]),
+        pltpu.make_async_copy(damping_hbm, damping, load_sem.at[7]),
+        pltpu.make_async_copy(profile_hbm, profile, load_sem.at[8]),
+    ]
     load_res.start()
+    load_counts.start()
     load_depth.start()
+    for copy in small:
+        copy.start()
     load_eta.start()
     load_flow.start()
     load_cell.start()
@@ -125,6 +139,7 @@
         )
 
     load_res.wait()
+    load_counts.wait()
     live_count = counts[pl.ds(own, 1), :]
     slot = lax.broadcasted_iota(jnp.int32, (half, tiles), 0)
     pieces = []
@@ -180,6 +195,8 @@
     def _():
         exchange()
 
+    for copy in small:
+        copy.wait()
     padded = level_rows.shape[1]
     level_rows[...] = jnp.zeros_like(level_rows)
     for level in range(levels):
@@ -297,6 +314,9 @@
     def _():
         exchange()
 
+    pl.semaphore_wait(half_in, 1)
+    tell(beside_in, before, win)
+    tell(beside_in, after, win)
     to_before.wait_recv()
     to_after.wait_recv()
     sub = lax.broadcasted_iota(jnp.int32, (SUB, LANES), 0)
@@ -319,44 +339,6 @@
                 value = jnp.where(classes == index, speed[index], value)
             celerity[j, k] = jnp.where(valid == 1, value, f32(0.0))
 
-    pl.semaphore_wait(half_in, 1)
-    tell(beside_in, before, win)
-    tell(beside_in, after, win)
-
-    pltpu.make_async_copy(
-        recv.at[pl.ds(0, tiles - 1)], recv.at[pl.ds(0, tiles - 1)], res_recv
-    ).wait()
-    values = recv[:, 0, :]
-    values = jnp.transpose(
-        jnp.concatenate([values, pltpu.roll(values, LANES // 2, axis=1)], axis=0)
-    )
-    cols[...] = values[: steps * half]
-    ring_rows = [(sub * PHASES + k).astype(f32) for k in range(PHASES)]
-
-    def expand(i, carry):
-        lanes = pl.ds(pl.multiple_of(i * LANES, LANES), LANES)
-        row = places[pl.ds(half + i, 1), :]
-        match = [row == ring_rows[k] for k in range(PHASES)]
-        high, low = [], []
-        for t in range(steps):
-            value = cols[pl.ds(t * half + i, 1), :]
-            coarse = value.astype(jnp.bfloat16).astype(f32)
-            fine = value - coarse
-            for k in range(PHASES):
-                high.append(jnp.where(match[k], coarse, f32(0.0)))
-                low.append(jnp.where(match[k], fine, f32(0.0)))
-        onehot_row[:, lanes] = jnp.concatenate(high + low, axis=0).astype(jnp.bfloat16)
-        return carry
-
-    lax.fori_loop(0, half, expand, 0, unroll=2)
-    product = lax.dot_general(
-        onehot_row[...],
-        onehot_col[...],
-        (((1,), (1,)), ((), ())),
-        preferred_element_type=f32,
-    )
-    inject[...] = product[: steps * RING] + product[steps * RING :]
-
     at_left = lane == 0
     at_right = lane == LANES - 1
     scale = f32(1.0 / math.sqrt(levels))
@@ -386,29 +368,72 @@
     def plus(x, y):
         return [[x[j][k] + y[j][k] for k in range(PHASES)] for j in range(blocks)]
 
+    top = laplace(field(len(slots)))
+    for s in range(1, steps + 1):
+        value = plus(field(place[s, s - 1]), top)
+        for power in range(s - 2, -1, -1):
+            value = plus(field(place[s, power]), laplace(value))
+        for j in range(blocks):
+            for k in range(PHASES):
+                from_state[s - 1, j, k] = value[j][k]
+
+    pltpu.make_async_copy(
+        recv.at[pl.ds(0, tiles - 1)], recv.at[pl.ds(0, tiles - 1)], res_recv
+    ).wait()
+    values = recv[:, 0, :]
+    values = jnp.transpose(
+        jnp.concatenate([values, pltpu.roll(values, LANES // 2, axis=1)], axis=0)
+    )
+    cols[...] = values[: steps * half]
+    ring_rows = [(sub * PHASES + k).astype(f32) for k in range(PHASES)]
+
+    def expand(i, carry):
+        lanes = pl.ds(pl.multiple_of(i * LANES, LANES), LANES)
+        row = places[pl.ds(half + i, 1), :]
+        match = [row == ring_rows[k] for k in range(PHASES)]
+        high, low = [], []
+        for t in range(steps):
+            value = cols[pl.ds(t * half + i, 1), :]
+            coarse = value.astype(jnp.bfloat16).astype(f32)
+            fine = value - coarse
+            for k in range(PHASES):
+                high.append(jnp.where(match[k], coarse, f32(0.0)))
+                low.append(jnp.where(match[k], fine, f32(0.0)))
+        onehot_row[:, lanes] = jnp.concatenate(high + low, axis=0).astype(jnp.bfloat16)
+        return carry
+
+    lax.fori_loop(0, half, expand, 0, unroll=4)
+    product = lax.dot_general(
+        onehot_row[...],
+        onehot_col[...],
+        (((1,), (1,)), ((), ())),
+        preferred_element_type=f32,
+    )
+    inject[...] = product[: steps * RING] + product[steps * RING :]
+
     def source(s, power):
-        value = field(place[s, power])
+        value = [[None] * PHASES for _ in range(blocks)]
         for n in range(1, s - power + 1):
             g = gammas[pl.ds(gamma_place[s - n, power], 1), :]
             t = steps - n
             for j in range(blocks):
                 for k in range(PHASES):
-                    value[j][k] = value[j][k] + g * inject[
+                    term = g * inject[
                         pl.ds((t * PHASES + k) * SUB, SUB), pl.ds(j * LANES, LANES)
                     ]
+                    value[j][k] = term if value[j][k] is None else value[j][k] + term
         return value
 
-    top = laplace(field(len(slots)))
     for s in range(1, steps + 1):
-        value = plus(source(s, s - 1), top)
+        value = source(s, s - 1)
         for power in range(s - 2, -1, -1):
             value = plus(source(s, power), laplace(value))
         t = steps - s
         for j in range(blocks):
             for k in range(PHASES):
                 send_rows[pl.ds(k * part + t * blocks + j, SUB, stride=PHASES * part), :] = (
-                    value[j][k] * scale
-                )
+                    value[j][k] + from_state[s - 1, j, k]
+                ) * scale
 
     slot_rows = pl.ds(pl.multiple_of(win * part, part), part)
     edge_copies = []
@@ -429,10 +454,6 @@
                     device_id_type=MESH,
                 )
             )
-    pl.semaphore_wait(beside_in, 2)
-    for copy in edge_copies:
-        copy.start()
-
     def send_row(target):
         pltpu.make_async_remote_copy(
             src_ref=send_rows.at[pl.ds(pl.multiple_of(target * part, part), part)],
@@ -452,6 +473,9 @@
         return carry
 
     lax.fori_loop(0, side, send_far, 0)
+    pl.semaphore_wait(beside_in, 2)
+    for copy in edge_copies:
+        copy.start()
     lax.fori_loop(1, side, send_near, 0)
     rows_in[slot_rows, :] = send_rows[slot_rows, :]
 
@@ -529,9 +553,13 @@
     total = pl.pallas_call(
         functools.partial(kernel, (tiles, windows, levels, rows, blocks, steps, cap)),
         out_shape=jax.ShapeDtypeStruct((length + TAIL, LANES), f32),
-        in_specs=[hbm, hbm, hbm, hbm, vmem, hbm, smem, smem, smem],
+        in_specs=[hbm] * 9,
         out_specs=vmem,
         scratch_shapes=[
+            pltpu.VMEM(sensor_count.shape, i32),
+            pltpu.SMEM(speed_table.shape, f32),
+            pltpu.SMEM(damping.shape, f32),
+            pltpu.SMEM(profile.shape, f32),
             pltpu.VMEM((levels, rows, across), f32),
             pltpu.VMEM((levels, rows, across), f32),
             pltpu.VMEM((2, padded, LANES), f32),
@@ -552,10 +580,11 @@
             pltpu.VMEM((cap, LANES), f32),
             pltpu.VMEM((steps * cap // 2, LANES), f32),
             pltpu.VMEM((steps * RING, across), f32),
+            pltpu.VMEM((steps, blocks, PHASES, SUB, LANES), f32),
             pltpu.VMEM((RING * part, LANES), f32),
             pltpu.VMEM((length, LANES), f32),
             pltpu.VMEM((length, LANES), f32),
-            dma((5,)),
+            dma((9,)),
             dma((2,)),
             dma((2,)),
             dma,

time: 43.9 us -> 42.8 us (0.975)
  Pallas kernels: 43.7 us -> 42.7 us
    pallas_call x1, Pallas kernels: 42 us -> 41 us  [body(): pl.pallas_call(functools.partial(kernel, (tiles, windows, levels, rows, b...]
where the time goes in v3:
time: 42.8 us; the launch traced here: 42.7 us
  Pallas kernels  42.7 us (100%)
    pallas_call x1, Pallas kernels, body(): pl.pallas_call(functools.partial(kernel, (tiles, windows, levels, rows, b...  41 us
    pallas_call x1, Pallas kernels, body(): pl.pallas_call(functools.partial(prior, blocks, length), out_shape=jax.Sh...  1.65 us

profile of v3, /device:TPU:1, one launch (start us, length us, event | category | flops | bytes accessed | tf_op | source)
XLA Modules:
  0.0 42.7 jit_solution(2476999743350739033)
XLA Ops:
  0.0 41.0 %adjoint.1.total = f32[288,128]{1,0:T(8,128)} custom-call(f32[30,16,512]{2,1,0:T(8,128)} %bitcast.10, f32[30,16,512]{2,1,0:T(8,128)} %bitcast.11, f32[128,64]{1,0:T(8,128)} %bitcast.12, s32[64,32,64]{2,1,0:T(8,128)} %bitcast.9, s32[64,64]{1,0:T(8,128)} %counts_hbm.1, s32[16,512]{1,0:T(8,128)} %depth.1, f32[8]{0:T(128)} %speed_hbm.1, f32[30]{0:T(128)} %damping_hbm.1, ...), custom_call_target="tpu_custom_call" | custom-call | tf_op jit(solution)/shard_map/adjoint/pallas_call | solution.py:553
  41.0 1.6 %prior.1 = f32[256,128]{1,0:T(8,128)} custom-call(f32[288,128]{1,0:T(8,128)} %adjoint.1.total, f32[8]{0:T(128)} %band.1), custom_call_target="tpu_custom_call" | custom-call | tf_op jit(solution)/shard_map/prior/pallas_call | solution.py:614

commit v4 on v3

--- a/solution.py
+++ b/solution.py
@@ -95,9 +95,6 @@
     load_depth.start()
     for copy in small:
         copy.start()
-    load_eta.start()
-    load_flow.start()
-    load_cell.start()
 
     edge_in[...] = jnp.zeros_like(edge_in)
     if tiles < SLOTS:
@@ -137,6 +134,10 @@
         pl.semaphore_signal(
             semaphore, inc=1, device_id={"trench": tile, "tblock": window}, device_id_type=MESH
         )
+
+    load_eta.start()
+    load_flow.start()
+    load_cell.start()
 
     load_res.wait()
     load_counts.wait()
@@ -402,7 +403,7 @@
         onehot_row[:, lanes] = jnp.concatenate(high + low, axis=0).astype(jnp.bfloat16)
         return carry
 
-    lax.fori_loop(0, half, expand, 0, unroll=4)
+    lax.fori_loop(0, half, expand, 0, unroll=8)
     product = lax.dot_general(
         onehot_row[...],
         onehot_col[...],

time: 42.8 us -> 42.8 us (level)
  no operation moved by 1% of the time
where the time goes in v4:
time: 42.8 us; the launch traced here: 42.7 us
  Pallas kernels  42.7 us (100%)
    pallas_call x1, Pallas kernels, body(): pl.pallas_call(functools.partial(kernel, (tiles, windows, levels, rows, b...  41 us
    pallas_call x1, Pallas kernels, body(): pl.pallas_call(functools.partial(prior, blocks, length), out_shape=jax.Sh...  1.65 us

profile of v4, /device:TPU:1, one launch (start us, length us, event | category | flops | bytes accessed | tf_op | source)
XLA Modules:
  0.0 42.7 jit_solution(2752718792283319347)
XLA Ops:
  0.0 41.0 %adjoint.1.total = f32[288,128]{1,0:T(8,128)} custom-call(f32[30,16,512]{2,1,0:T(8,128)} %bitcast.10, f32[30,16,512]{2,1,0:T(8,128)} %bitcast.11, f32[128,64]{1,0:T(8,128)} %bitcast.12, s32[64,32,64]{2,1,0:T(8,128)} %bitcast.9, s32[64,64]{1,0:T(8,128)} %counts_hbm.1, s32[16,512]{1,0:T(8,128)} %depth.1, f32[8]{0:T(128)} %speed_hbm.1, f32[30]{0:T(128)} %damping_hbm.1, ...), custom_call_target="tpu_custom_call" | custom-call | tf_op jit(solution)/shard_map/adjoint/pallas_call | solution.py:554
  41.0 1.6 %prior.1 = f32[256,128]{1,0:T(8,128)} custom-call(f32[288,128]{1,0:T(8,128)} %adjoint.1.total, f32[8]{0:T(128)} %band.1), custom_call_target="tpu_custom_call" | custom-call | tf_op jit(solution)/shard_map/prior/pallas_call | solution.py:615
